TPU v7x, 32 devices: a whole 2x2x4 slice. The times are simulated.
32 devices in a mesh: section: 4 (over x, core), blk: 8 (over z, y).
Axes of the slice: x: 2, y: 2, z: 4, core: 2. Of those that a mesh axis runs over, the one named last changes fastest.
Arguments:
- features: bfloat16 [4, 3072, 256], P(None, 'blk'), may hold values from -6 to 6
- pattern: int32 [4, 24, 3, 128, 128], P(None, 'blk'), may hold values 0 or 1
- col_block: int32 [4, 24, 3], P(None, 'blk'), may hold values from 0 to 23, as said below
- degree: int32 [4, 3072], P(None, 'blk'), may hold values from 4 to 24
- weight: bfloat16 [4, 256, 256], P('section'), may hold values from -0.375 to 0.375
- bias: float32 [4, 256], P('section'), may hold values from -3 to 3
Outputs:
- embeddings: bfloat16 [4, 3072, 256], P('section', 'blk')
Inputs may be any that keep to these rules, and one draw needn't show every extreme that they name: col_block[c, b, k] lies within 1 block of b: slot 0 is b - 1 and slot 2 is b + 1, both clipped to the subgraph's blocks; the middle slots are anywhere in that range.
All inputs are finite; a program needn't handle non-finite values. No bound on the sum of `pattern` on one device may be relied on, other than what follows from the above.
Results may differ from a plain program's by a relative error of at most 0.012.
Values may be sent and summed in bfloat16 or wider, within the bound.
A program may use at most 64 MiB of HBM per device.

v0:
```python
import jax
import jax.numpy as jnp
from jax import lax
from jax.sharding import PartitionSpec as P

REACH = 1


def extended(block, sides, width):
    for axis, dim in sides:
        count = lax.axis_size(axis)
        forward = [(i, i + 1) for i in range(count - 1)]
        backward = [(target, source) for source, target in forward]
        low = lax.ppermute(
            lax.slice_in_dim(block, block.shape[dim] - width, None, axis=dim), axis, forward
        )
        high = lax.ppermute(lax.slice_in_dim(block, 0, width, axis=dim), axis, backward)
        block = jnp.concatenate([low, block, high], axis=dim)
    return block


def passed_along(block, axis, distance):
    devices = range(lax.axis_size(axis))
    route = [(i - distance, i) for i in devices if i - distance in devices]
    return lax.ppermute(block, axis, route)


def shards(features, pattern, col_block, degree, weight, bias):
    sections = lax.axis_size("section")
    groups = features.shape[0]
    slab_rows = features.shape[1]
    feat_width = features.shape[2]
    per_dev = pattern.shape[1]
    tile_rows = pattern.shape[-1]
    section_idx = lax.axis_index("section")
    first_block = lax.axis_index("blk") * per_dev

    def apply_layer(current, group_now, layer_weight, layer_bias):
        degrees = lax.dynamic_index_in_dim(degree, group_now, 0, keepdims=False)
        inv_root = lax.rsqrt(degrees.astype(jnp.float32))[:, None]
        scaled = (current.astype(jnp.float32) * inv_root).astype(jnp.bfloat16)
        tile_ones = lax.dynamic_index_in_dim(pattern, group_now, 0, keepdims=False).astype(
            jnp.bfloat16
        )
        column_ids = (
            lax.dynamic_index_in_dim(col_block, group_now, 0, keepdims=False) - first_block + REACH
        )
        own_blocks = scaled.reshape(per_dev, tile_rows, feat_width)
        padded = extended(scaled, (("blk", 0),), REACH * tile_rows)
        padded_blocks = padded.reshape(per_dev + 2 * REACH, tile_rows, feat_width)
        sources = jnp.take(padded_blocks, column_ids, axis=0)
        summed = jnp.einsum(
            "bkij,bkjf->bif", tile_ones, sources, preferred_element_type=jnp.float32
        )
        summed = summed + own_blocks.astype(jnp.float32)
        aggregate = (summed.reshape(slab_rows, feat_width) * inv_root).astype(jnp.bfloat16)
        hidden = jnp.dot(aggregate, layer_weight, preferred_element_type=jnp.float32) + layer_bias
        return (current.astype(jnp.float32) + jax.nn.relu(hidden)).astype(jnp.bfloat16)

    layer_weight = weight[0]
    layer_bias = bias[0]

    def relay_step(clock, carry):
        incoming, finished_rows = carry
        group_now = jnp.clip(clock - section_idx, 0, groups - 1)
        arriving = lax.dynamic_index_in_dim(
            features, jnp.clip(clock, 0, groups - 1), 0, keepdims=False
        )
        current = jnp.where(section_idx == 0, arriving, incoming)
        updated = apply_layer(current, group_now, layer_weight, layer_bias)
        finish_idx = clock - (sections - 1)
        is_last = (section_idx == sections - 1) & (finish_idx >= 0)
        finish_slot = jnp.clip(finish_idx, 0, groups - 1)
        previous = lax.dynamic_index_in_dim(finished_rows, finish_slot, 0, keepdims=True)
        chosen = jnp.where(is_last, updated[None], previous)
        finished_rows = lax.dynamic_update_index_in_dim(finished_rows, chosen, finish_slot, 0)
        incoming = passed_along(updated, "section", 1)
        return (incoming, finished_rows)

    start_rows = jnp.zeros((slab_rows, feat_width), jnp.bfloat16)
    start_done = jnp.zeros((groups, slab_rows, feat_width), jnp.bfloat16)
    incoming, finished_rows = lax.fori_loop(
        0, groups + sections - 1, relay_step, (start_rows, start_done)
    )
    received = lax.all_to_all(finished_rows, "section", split_axis=0, concat_axis=0, tiled=True)
    return received[sections - 1 : sections]


def solution(mesh):
    return jax.shard_map(
        shards,
        mesh=mesh,
        in_specs=(
            P(None, "blk", None),
            P(None, "blk", None, None, None),
            P(None, "blk", None),
            P(None, "blk"),
            P("section", None, None),
            P("section", None),
        ),
        out_specs=P("section", "blk", None),
        check_vma=False,
    )
```

profile of v0, /device:TPU:24, one launch (start us, length us, event | category | flops | bytes accessed | tf_op | source)
XLA Modules:
  0.0 167.3 jit_solution(7323270041476663340)
XLA Ops:
  0.1 146.3 %while.17 = (s32[]{:T(128)}, bf16[384,256]{1,0:T(8,128)(2,1)S(1)}, bf16[4,384,256]{2,1,0:T(8,128)(2,1)S(1)}, pred[]{:T(512)}, bf16[4,384,256]{2,1,0:T(8,128)(2,1...) while((s32[]{:T(128)}, bf16[384,256]{1,0:T(8,128)(2,1)S(1)}, ...), condition=%wide.region_1.2_spmd, body=%wide.region_0.1_spmd.sunk | while | flops 128730600 | bytes 8208210 | solution.py:82
  1.9 3.4 %collective-permute-start = (bf16[128,256]{1,0:T(8,128)(2,1)S(1)}, bf16[128,256]{1,0:T(8,128)(2,1)S(1)}, u32[]{:S(2)}, u32[]{:S(2)}) collective-permute-start(bf16[128,256]{1,0:T(8,128)(2,1)S(1)} %get-tuple-element.401), channel_id=1, source_target_pairs={{1,0},{2,1},{3,2},{4,3},{5,4},{6,5},{7,6},{9,8},{10,9},{11,10},{12... | collective-permute-start | bytes 196616 | tf_op jit(solution)/shard_map/while/body/eval_jaxpr/ppermute | solution.py:17
  5.4 2.5 %collective-permute-start.1 = (bf16[128,256]{1,0:T(8,128)(2,1)S(1)}, bf16[128,256]{1,0:T(8,128)(2,1)S(1)}, u32[]{:S(2)}, u32[]{:S(2)}) collective-permute-start(bf16[128,256]{1,0:T(8,128)(2,1)S(1)} %get-tuple-element.402), channel_id=1, source_target_pairs={{0,1},{1,2},{2,3},{3,4},{4,5},{5,6},{6,7},{8,9},{9,10},{10,11},{11... | collective-permute-start | bytes 196616 | tf_op jit(solution)/shard_map/while/body/eval_jaxpr/ppermute | solution.py:14
  8.8 3.7 %collective-permute-done.1 = bf16[128,256]{1,0:T(8,128)(2,1)S(1)} collective-permute-done((bf16[128,256]{1,0:T(8,128)(2,1)S(1)}, bf16[128,256]{1,0:T(8,128)(2,1)S(1)}, u32[]{:S(2)}, u32[]{:S(2)}) %collective-permute-start.1) | collective-permute-done | bytes 65568 | tf_op jit(solution)/shard_map/while/body/eval_jaxpr/ppermute | solution.py:14
  20.0 2.1 %collective-permute-start = (bf16[128,256]{1,0:T(8,128)(2,1)S(1)}, bf16[128,256]{1,0:T(8,128)(2,1)S(1)}, u32[]{:S(2)}, u32[]{:S(2)}) collective-permute-start(bf16[128,256]{1,0:T(8,128)(2,1)S(1)} %get-tuple-element.401), channel_id=1, source_target_pairs={{1,0},{2,1},{3,2},{4,3},{5,4},{6,5},{7,6},{9,8},{10,9},{11,10},{12... | collective-permute-start | bytes 196616 | tf_op jit(solution)/shard_map/while/body/eval_jaxpr/ppermute | solution.py:17
  22.0 3.9 %collective-permute-start.1 = (bf16[128,256]{1,0:T(8,128)(2,1)S(1)}, bf16[128,256]{1,0:T(8,128)(2,1)S(1)}, u32[]{:S(2)}, u32[]{:S(2)}) collective-permute-start(bf16[128,256]{1,0:T(8,128)(2,1)S(1)} %get-tuple-element.402), channel_id=1, source_target_pairs={{0,1},{1,2},{2,3},{3,4},{4,5},{5,6},{6,7},{8,9},{9,10},{10,11},{11... | collective-permute-start | bytes 196616 | tf_op jit(solution)/shard_map/while/body/eval_jaxpr/ppermute | solution.py:14
  26.8 2.4 %collective-permute-done.1 = bf16[128,256]{1,0:T(8,128)(2,1)S(1)} collective-permute-done((bf16[128,256]{1,0:T(8,128)(2,1)S(1)}, bf16[128,256]{1,0:T(8,128)(2,1)S(1)}, u32[]{:S(2)}, u32[]{:S(2)}) %collective-permute-start.1) | collective-permute-done | bytes 65568 | tf_op jit(solution)/shard_map/while/body/eval_jaxpr/ppermute | solution.py:14
  29.8 1.4 fusion.35
  32.5 4.4 %collective-permute-start.2 = (bf16[384,256]{1,0:T(8,128)(2,1)S(1)}, bf16[384,256]{1,0:T(8,128)(2,1)S(1)}, u32[]{:S(2)}, u32[]{:S(2)}) collective-permute-start(bf16[384,256]{1,0:T(8,128)(2,1)S(1)} %get-tuple-element.406), channel_id=1, source_target_pairs={{0,8},{8,16},{16,24},{1,9},{9,17},{17,25},{2,10},{10,18},{18,26},{... | collective-permute-start | bytes 589832 | tf_op jit(solution)/shard_map/while/body/eval_jaxpr/ppermute | solution.py:25
  39.8 2.8 %collective-permute-start = (bf16[128,256]{1,0:T(8,128)(2,1)S(1)}, bf16[128,256]{1,0:T(8,128)(2,1)S(1)}, u32[]{:S(2)}, u32[]{:S(2)}) collective-permute-start(bf16[128,256]{1,0:T(8,128)(2,1)S(1)} %get-tuple-element.401), channel_id=1, source_target_pairs={{1,0},{2,1},{3,2},{4,3},{5,4},{6,5},{7,6},{9,8},{10,9},{11,10},{12... | collective-permute-start | bytes 196616 | tf_op jit(solution)/shard_map/while/body/eval_jaxpr/ppermute | solution.py:17
  42.6 3.2 %collective-permute-start.1 = (bf16[128,256]{1,0:T(8,128)(2,1)S(1)}, bf16[128,256]{1,0:T(8,128)(2,1)S(1)}, u32[]{:S(2)}, u32[]{:S(2)}) collective-permute-start(bf16[128,256]{1,0:T(8,128)(2,1)S(1)} %get-tuple-element.402), channel_id=1, source_target_pairs={{0,1},{1,2},{2,3},{3,4},{4,5},{5,6},{6,7},{8,9},{9,10},{10,11},{11... | collective-permute-start | bytes 196616 | tf_op jit(solution)/shard_map/while/body/eval_jaxpr/ppermute | solution.py:14
  46.7 3.0 %collective-permute-done.1 = bf16[128,256]{1,0:T(8,128)(2,1)S(1)} collective-permute-done((bf16[128,256]{1,0:T(8,128)(2,1)S(1)}, bf16[128,256]{1,0:T(8,128)(2,1)S(1)}, u32[]{:S(2)}, u32[]{:S(2)}) %collective-permute-start.1) | collective-permute-done | bytes 65568 | tf_op jit(solution)/shard_map/while/body/eval_jaxpr/ppermute | solution.py:14
  50.3 1.4 fusion.35
  53.0 5.9 %collective-permute-start.2 = (bf16[384,256]{1,0:T(8,128)(2,1)S(1)}, bf16[384,256]{1,0:T(8,128)(2,1)S(1)}, u32[]{:S(2)}, u32[]{:S(2)}) collective-permute-start(bf16[384,256]{1,0:T(8,128)(2,1)S(1)} %get-tuple-element.406), channel_id=1, source_target_pairs={{0,8},{8,16},{16,24},{1,9},{9,17},{17,25},{2,10},{10,18},{18,26},{... | collective-permute-start | bytes 589832 | tf_op jit(solution)/shard_map/while/body/eval_jaxpr/ppermute | solution.py:25
  61.8 2.1 %collective-permute-start = (bf16[128,256]{1,0:T(8,128)(2,1)S(1)}, bf16[128,256]{1,0:T(8,128)(2,1)S(1)}, u32[]{:S(2)}, u32[]{:S(2)}) collective-permute-start(bf16[128,256]{1,0:T(8,128)(2,1)S(1)} %get-tuple-element.401), channel_id=1, source_target_pairs={{1,0},{2,1},{3,2},{4,3},{5,4},{6,5},{7,6},{9,8},{10,9},{11,10},{12... | collective-permute-start | bytes 196616 | tf_op jit(solution)/shard_map/while/body/eval_jaxpr/ppermute | solution.py:17
  63.9 3.9 %collective-permute-start.1 = (bf16[128,256]{1,0:T(8,128)(2,1)S(1)}, bf16[128,256]{1,0:T(8,128)(2,1)S(1)}, u32[]{:S(2)}, u32[]{:S(2)}) collective-permute-start(bf16[128,256]{1,0:T(8,128)(2,1)S(1)} %get-tuple-element.402), channel_id=1, source_target_pairs={{0,1},{1,2},{2,3},{3,4},{4,5},{5,6},{6,7},{8,9},{9,10},{10,11},{11... | collective-permute-start | bytes 196616 | tf_op jit(solution)/shard_map/while/body/eval_jaxpr/ppermute | solution.py:14
  68.7 2.3 %collective-permute-done.1 = bf16[128,256]{1,0:T(8,128)(2,1)S(1)} collective-permute-done((bf16[128,256]{1,0:T(8,128)(2,1)S(1)}, bf16[128,256]{1,0:T(8,128)(2,1)S(1)}, u32[]{:S(2)}, u32[]{:S(2)}) %collective-permute-start.1) | collective-permute-done | bytes 65568 | tf_op jit(solution)/shard_map/while/body/eval_jaxpr/ppermute | solution.py:14
  71.6 1.4 fusion.35
  74.3 6.2 %collective-permute-start.2 = (bf16[384,256]{1,0:T(8,128)(2,1)S(1)}, bf16[384,256]{1,0:T(8,128)(2,1)S(1)}, u32[]{:S(2)}, u32[]{:S(2)}) collective-permute-start(bf16[384,256]{1,0:T(8,128)(2,1)S(1)} %get-tuple-element.406), channel_id=1, source_target_pairs={{0,8},{8,16},{16,24},{1,9},{9,17},{17,25},{2,10},{10,18},{18,26},{... | collective-permute-start | bytes 589832 | tf_op jit(solution)/shard_map/while/body/eval_jaxpr/ppermute | solution.py:25
  83.4 2.8 %collective-permute-start = (bf16[128,256]{1,0:T(8,128)(2,1)S(1)}, bf16[128,256]{1,0:T(8,128)(2,1)S(1)}, u32[]{:S(2)}, u32[]{:S(2)}) collective-permute-start(bf16[128,256]{1,0:T(8,128)(2,1)S(1)} %get-tuple-element.401), channel_id=1, source_target_pairs={{1,0},{2,1},{3,2},{4,3},{5,4},{6,5},{7,6},{9,8},{10,9},{11,10},{12... | collective-permute-start | bytes 196616 | tf_op jit(solution)/shard_map/while/body/eval_jaxpr/ppermute | solution.py:17
  86.1 3.2 %collective-permute-start.1 = (bf16[128,256]{1,0:T(8,128)(2,1)S(1)}, bf16[128,256]{1,0:T(8,128)(2,1)S(1)}, u32[]{:S(2)}, u32[]{:S(2)}) collective-permute-start(bf16[128,256]{1,0:T(8,128)(2,1)S(1)} %get-tuple-element.402), channel_id=1, source_target_pairs={{0,1},{1,2},{2,3},{3,4},{4,5},{5,6},{6,7},{8,9},{9,10},{10,11},{11... | collective-permute-start | bytes 196616 | tf_op jit(solution)/shard_map/while/body/eval_jaxpr/ppermute | solution.py:14
  90.2 3.0 %collective-permute-done.1 = bf16[128,256]{1,0:T(8,128)(2,1)S(1)} collective-permute-done((bf16[128,256]{1,0:T(8,128)(2,1)S(1)}, bf16[128,256]{1,0:T(8,128)(2,1)S(1)}, u32[]{:S(2)}, u32[]{:S(2)}) %collective-permute-start.1) | collective-permute-done | bytes 65568 | tf_op jit(solution)/shard_map/while/body/eval_jaxpr/ppermute | solution.py:14
  96.6 5.9 %collective-permute-start.2 = (bf16[384,256]{1,0:T(8,128)(2,1)S(1)}, bf16[384,256]{1,0:T(8,128)(2,1)S(1)}, u32[]{:S(2)}, u32[]{:S(2)}) collective-permute-start(bf16[384,256]{1,0:T(8,128)(2,1)S(1)} %get-tuple-element.406), channel_id=1, source_target_pairs={{0,8},{8,16},{16,24},{1,9},{9,17},{17,25},{2,10},{10,18},{18,26},{... | collective-permute-start | bytes 589832 | tf_op jit(solution)/shard_map/while/body/eval_jaxpr/ppermute | solution.py:25
  105.4 2.1 %collective-permute-start = (bf16[128,256]{1,0:T(8,128)(2,1)S(1)}, bf16[128,256]{1,0:T(8,128)(2,1)S(1)}, u32[]{:S(2)}, u32[]{:S(2)}) collective-permute-start(bf16[128,256]{1,0:T(8,128)(2,1)S(1)} %get-tuple-element.401), channel_id=1, source_target_pairs={{1,0},{2,1},{3,2},{4,3},{5,4},{6,5},{7,6},{9,8},{10,9},{11,10},{12... | collective-permute-start | bytes 196616 | tf_op jit(solution)/shard_map/while/body/eval_jaxpr/ppermute | solution.py:17
  107.4 3.9 %collective-permute-start.1 = (bf16[128,256]{1,0:T(8,128)(2,1)S(1)}, bf16[128,256]{1,0:T(8,128)(2,1)S(1)}, u32[]{:S(2)}, u32[]{:S(2)}) collective-permute-start(bf16[128,256]{1,0:T(8,128)(2,1)S(1)} %get-tuple-element.402), channel_id=1, source_target_pairs={{0,1},{1,2},{2,3},{3,4},{4,5},{5,6},{6,7},{8,9},{9,10},{10,11},{11... | collective-permute-start | bytes 196616 | tf_op jit(solution)/shard_map/while/body/eval_jaxpr/ppermute | solution.py:14
  112.2 2.3 %collective-permute-done.1 = bf16[128,256]{1,0:T(8,128)(2,1)S(1)} collective-permute-done((bf16[128,256]{1,0:T(8,128)(2,1)S(1)}, bf16[128,256]{1,0:T(8,128)(2,1)S(1)}, u32[]{:S(2)}, u32[]{:S(2)}) %collective-permute-start.1) | collective-permute-done | bytes 65568 | tf_op jit(solution)/shard_map/while/body/eval_jaxpr/ppermute | solution.py:14
  117.8 6.2 %collective-permute-start.2 = (bf16[384,256]{1,0:T(8,128)(2,1)S(1)}, bf16[384,256]{1,0:T(8,128)(2,1)S(1)}, u32[]{:S(2)}, u32[]{:S(2)}) collective-permute-start(bf16[384,256]{1,0:T(8,128)(2,1)S(1)} %get-tuple-element.406), channel_id=1, source_target_pairs={{0,8},{8,16},{16,24},{1,9},{9,17},{17,25},{2,10},{10,18},{18,26},{... | collective-permute-start | bytes 589832 | tf_op jit(solution)/shard_map/while/body/eval_jaxpr/ppermute | solution.py:25
  126.9 2.1 %collective-permute-start = (bf16[128,256]{1,0:T(8,128)(2,1)S(1)}, bf16[128,256]{1,0:T(8,128)(2,1)S(1)}, u32[]{:S(2)}, u32[]{:S(2)}) collective-permute-start(bf16[128,256]{1,0:T(8,128)(2,1)S(1)} %get-tuple-element.401), channel_id=1, source_target_pairs={{1,0},{2,1},{3,2},{4,3},{5,4},{6,5},{7,6},{9,8},{10,9},{11,10},{12... | collective-permute-start | bytes 196616 | tf_op jit(solution)/shard_map/while/body/eval_jaxpr/ppermute | solution.py:17
  129.0 3.9 %collective-permute-start.1 = (bf16[128,256]{1,0:T(8,128)(2,1)S(1)}, bf16[128,256]{1,0:T(8,128)(2,1)S(1)}, u32[]{:S(2)}, u32[]{:S(2)}) collective-permute-start(bf16[128,256]{1,0:T(8,128)(2,1)S(1)} %get-tuple-element.402), channel_id=1, source_target_pairs={{0,1},{1,2},{2,3},{3,4},{4,5},{5,6},{6,7},{8,9},{9,10},{10,11},{11... | collective-permute-start | bytes 196616 | tf_op jit(solution)/shard_map/while/body/eval_jaxpr/ppermute | solution.py:14
  133.8 2.3 %collective-permute-done.1 = bf16[128,256]{1,0:T(8,128)(2,1)S(1)} collective-permute-done((bf16[128,256]{1,0:T(8,128)(2,1)S(1)}, bf16[128,256]{1,0:T(8,128)(2,1)S(1)}, u32[]{:S(2)}, u32[]{:S(2)}) %collective-permute-start.1) | collective-permute-done | bytes 65568 | tf_op jit(solution)/shard_map/while/body/eval_jaxpr/ppermute | solution.py:14
  139.4 5.9 %collective-permute-start.2 = (bf16[384,256]{1,0:T(8,128)(2,1)S(1)}, bf16[384,256]{1,0:T(8,128)(2,1)S(1)}, u32[]{:S(2)}, u32[]{:S(2)}) collective-permute-start(bf16[384,256]{1,0:T(8,128)(2,1)S(1)} %get-tuple-element.406), channel_id=1, source_target_pairs={{0,8},{8,16},{16,24},{1,9},{9,17},{17,25},{2,10},{10,18},{18,26},{... | collective-permute-start | bytes 589832 | tf_op jit(solution)/shard_map/while/body/eval_jaxpr/ppermute | solution.py:25
  146.4 20.3 %all_to_all.5 = bf16[4,384,256]{2,1,0:T(8,128)(2,1)S(1)} all-to-all(bf16[4,384,256]{2,1,0:T(8,128)(2,1)S(1)} %get-tuple-element.281), channel_id=1, replica_groups=mesh['section'=4,'blk'=8] {'section'}, dimensions={0} | all-to-all | bytes 1572864 | tf_op jit(solution)/shard_map/all_to_all | solution.py:85
  (127 shorter events, 46.5 us)
Async XLA Ops:
  1.9 12.7 %copy-start = (bf16[256,256]{1,0:T(8,128)(2,1)S(1)}, bf16[256,256]{1,0:T(8,128)(2,1)}, u32[]{:S(2)}) copy-start(bf16[256,256]{1,0:T(8,128)(2,1)} %get-tuple-element.452) | copy-start | bytes 393220 | tf_op jit(solution)/shard_map/while
  1.9 12.7 %copy-start.1 = (f32[1,256]{1,0:T(1,128)S(1)}, f32[1,256]{1,0:T(1,128)}, u32[]{:S(2)}) copy-start(f32[1,256]{1,0:T(1,128)} %get-tuple-element.453) | copy-start | bytes 3076 | tf_op jit(solution)/shard_map/while
  1.9 6.8 %collective-permute-start = (bf16[128,256]{1,0:T(8,128)(2,1)S(1)}, bf16[128,256]{1,0:T(8,128)(2,1)S(1)}, u32[]{:S(2)}, u32[]{:S(2)}) collective-permute-start(bf16[128,256]{1,0:T(8,128)(2,1)S(1)} %get-tuple-element.401), channel_id=1, source_target_pairs={{1,0},{2,1},{3,2},{4,3},{5,4},{6,5},{7,6},{9,8},{10,9},{11,10},{12... | collective-permute-start | bytes 196616 | tf_op jit(solution)/shard_map/while/body/eval_jaxpr/ppermute | solution.py:17
  5.4 7.1 %collective-permute-start.1 = (bf16[128,256]{1,0:T(8,128)(2,1)S(1)}, bf16[128,256]{1,0:T(8,128)(2,1)S(1)}, u32[]{:S(2)}, u32[]{:S(2)}) collective-permute-start(bf16[128,256]{1,0:T(8,128)(2,1)S(1)} %get-tuple-element.402), channel_id=1, source_target_pairs={{0,1},{1,2},{2,3},{3,4},{4,5},{5,6},{6,7},{8,9},{9,10},{10,11},{11... | collective-permute-start | bytes 196616 | tf_op jit(solution)/shard_map/while/body/eval_jaxpr/ppermute | solution.py:14
  15.8 2.4 %collective-permute-start.2 = (bf16[384,256]{1,0:T(8,128)(2,1)S(1)}, bf16[384,256]{1,0:T(8,128)(2,1)S(1)}, u32[]{:S(2)}, u32[]{:S(2)}) collective-permute-start(bf16[384,256]{1,0:T(8,128)(2,1)S(1)} %get-tuple-element.406), channel_id=1, source_target_pairs={{0,8},{8,16},{16,24},{1,9},{9,17},{17,25},{2,10},{10,18},{18,26},{... | collective-permute-start | bytes 589832 | tf_op jit(solution)/shard_map/while/body/eval_jaxpr/ppermute | solution.py:25
  19.9 11.4 %copy-start = (bf16[256,256]{1,0:T(8,128)(2,1)S(1)}, bf16[256,256]{1,0:T(8,128)(2,1)}, u32[]{:S(2)}) copy-start(bf16[256,256]{1,0:T(8,128)(2,1)} %get-tuple-element.452) | copy-start | bytes 393220 | tf_op jit(solution)/shard_map/while
  19.9 11.4 %copy-start.1 = (f32[1,256]{1,0:T(1,128)S(1)}, f32[1,256]{1,0:T(1,128)}, u32[]{:S(2)}) copy-start(f32[1,256]{1,0:T(1,128)} %get-tuple-element.453) | copy-start | bytes 3076 | tf_op jit(solution)/shard_map/while
  20.0 6.8 %collective-permute-start = (bf16[128,256]{1,0:T(8,128)(2,1)S(1)}, bf16[128,256]{1,0:T(8,128)(2,1)S(1)}, u32[]{:S(2)}, u32[]{:S(2)}) collective-permute-start(bf16[128,256]{1,0:T(8,128)(2,1)S(1)} %get-tuple-element.401), channel_id=1, source_target_pairs={{1,0},{2,1},{3,2},{4,3},{5,4},{6,5},{7,6},{9,8},{10,9},{11,10},{12... | collective-permute-start | bytes 196616 | tf_op jit(solution)/shard_map/while/body/eval_jaxpr/ppermute | solution.py:17
  22.0 7.2 %collective-permute-start.1 = (bf16[128,256]{1,0:T(8,128)(2,1)S(1)}, bf16[128,256]{1,0:T(8,128)(2,1)S(1)}, u32[]{:S(2)}, u32[]{:S(2)}) collective-permute-start(bf16[128,256]{1,0:T(8,128)(2,1)S(1)} %get-tuple-element.402), channel_id=1, source_target_pairs={{0,1},{1,2},{2,3},{3,4},{4,5},{5,6},{6,7},{8,9},{9,10},{10,11},{11... | collective-permute-start | bytes 196616 | tf_op jit(solution)/shard_map/while/body/eval_jaxpr/ppermute | solution.py:14
  32.5 5.5 %collective-permute-start.2 = (bf16[384,256]{1,0:T(8,128)(2,1)S(1)}, bf16[384,256]{1,0:T(8,128)(2,1)S(1)}, u32[]{:S(2)}, u32[]{:S(2)}) collective-permute-start(bf16[384,256]{1,0:T(8,128)(2,1)S(1)} %get-tuple-element.406), channel_id=1, source_target_pairs={{0,8},{8,16},{16,24},{1,9},{9,17},{17,25},{2,10},{10,18},{18,26},{... | collective-permute-start | bytes 589832 | tf_op jit(solution)/shard_map/while/body/eval_jaxpr/ppermute | solution.py:25
  39.8 12.0 %copy-start = (bf16[256,256]{1,0:T(8,128)(2,1)S(1)}, bf16[256,256]{1,0:T(8,128)(2,1)}, u32[]{:S(2)}) copy-start(bf16[256,256]{1,0:T(8,128)(2,1)} %get-tuple-element.452) | copy-start | bytes 393220 | tf_op jit(solution)/shard_map/while
  39.8 12.0 %copy-start.1 = (f32[1,256]{1,0:T(1,128)S(1)}, f32[1,256]{1,0:T(1,128)}, u32[]{:S(2)}) copy-start(f32[1,256]{1,0:T(1,128)} %get-tuple-element.453) | copy-start | bytes 3076 | tf_op jit(solution)/shard_map/while
  39.8 6.8 %collective-permute-start = (bf16[128,256]{1,0:T(8,128)(2,1)S(1)}, bf16[128,256]{1,0:T(8,128)(2,1)S(1)}, u32[]{:S(2)}, u32[]{:S(2)}) collective-permute-start(bf16[128,256]{1,0:T(8,128)(2,1)S(1)} %get-tuple-element.401), channel_id=1, source_target_pairs={{1,0},{2,1},{3,2},{4,3},{5,4},{6,5},{7,6},{9,8},{10,9},{11,10},{12... | collective-permute-start | bytes 196616 | tf_op jit(solution)/shard_map/while/body/eval_jaxpr/ppermute | solution.py:17
  42.6 7.1 %collective-permute-start.1 = (bf16[128,256]{1,0:T(8,128)(2,1)S(1)}, bf16[128,256]{1,0:T(8,128)(2,1)S(1)}, u32[]{:S(2)}, u32[]{:S(2)}) collective-permute-start(bf16[128,256]{1,0:T(8,128)(2,1)S(1)} %get-tuple-element.402), channel_id=1, source_target_pairs={{0,1},{1,2},{2,3},{3,4},{4,5},{5,6},{6,7},{8,9},{9,10},{10,11},{11... | collective-permute-start | bytes 196616 | tf_op jit(solution)/shard_map/while/body/eval_jaxpr/ppermute | solution.py:14
  53.0 7.0 %collective-permute-start.2 = (bf16[384,256]{1,0:T(8,128)(2,1)S(1)}, bf16[384,256]{1,0:T(8,128)(2,1)S(1)}, u32[]{:S(2)}, u32[]{:S(2)}) collective-permute-start(bf16[384,256]{1,0:T(8,128)(2,1)S(1)} %get-tuple-element.406), channel_id=1, source_target_pairs={{0,8},{8,16},{16,24},{1,9},{9,17},{17,25},{2,10},{10,18},{18,26},{... | collective-permute-start | bytes 589832 | tf_op jit(solution)/shard_map/while/body/eval_jaxpr/ppermute | solution.py:25
  61.8 11.3 %copy-start = (bf16[256,256]{1,0:T(8,128)(2,1)S(1)}, bf16[256,256]{1,0:T(8,128)(2,1)}, u32[]{:S(2)}) copy-start(bf16[256,256]{1,0:T(8,128)(2,1)} %get-tuple-element.452) | copy-start | bytes 393220 | tf_op jit(solution)/shard_map/while
  61.8 11.3 %copy-start.1 = (f32[1,256]{1,0:T(1,128)S(1)}, f32[1,256]{1,0:T(1,128)}, u32[]{:S(2)}) copy-start(f32[1,256]{1,0:T(1,128)} %get-tuple-element.453) | copy-start | bytes 3076 | tf_op jit(solution)/shard_map/while
  61.8 6.8 %collective-permute-start = (bf16[128,256]{1,0:T(8,128)(2,1)S(1)}, bf16[128,256]{1,0:T(8,128)(2,1)S(1)}, u32[]{:S(2)}, u32[]{:S(2)}) collective-permute-start(bf16[128,256]{1,0:T(8,128)(2,1)S(1)} %get-tuple-element.401), channel_id=1, source_target_pairs={{1,0},{2,1},{3,2},{4,3},{5,4},{6,5},{7,6},{9,8},{10,9},{11,10},{12... | collective-permute-start | bytes 196616 | tf_op jit(solution)/shard_map/while/body/eval_jaxpr/ppermute | solution.py:17
  63.9 7.1 %collective-permute-start.1 = (bf16[128,256]{1,0:T(8,128)(2,1)S(1)}, bf16[128,256]{1,0:T(8,128)(2,1)S(1)}, u32[]{:S(2)}, u32[]{:S(2)}) collective-permute-start(bf16[128,256]{1,0:T(8,128)(2,1)S(1)} %get-tuple-element.402), channel_id=1, source_target_pairs={{0,1},{1,2},{2,3},{3,4},{4,5},{5,6},{6,7},{8,9},{9,10},{10,11},{11... | collective-permute-start | bytes 196616 | tf_op jit(solution)/shard_map/while/body/eval_jaxpr/ppermute | solution.py:14
  74.3 7.3 %collective-permute-start.2 = (bf16[384,256]{1,0:T(8,128)(2,1)S(1)}, bf16[384,256]{1,0:T(8,128)(2,1)S(1)}, u32[]{:S(2)}, u32[]{:S(2)}) collective-permute-start(bf16[384,256]{1,0:T(8,128)(2,1)S(1)} %get-tuple-element.406), channel_id=1, source_target_pairs={{0,8},{8,16},{16,24},{1,9},{9,17},{17,25},{2,10},{10,18},{18,26},{... | collective-permute-start | bytes 589832 | tf_op jit(solution)/shard_map/while/body/eval_jaxpr/ppermute | solution.py:25
  83.3 12.0 %copy-start = (bf16[256,256]{1,0:T(8,128)(2,1)S(1)}, bf16[256,256]{1,0:T(8,128)(2,1)}, u32[]{:S(2)}) copy-start(bf16[256,256]{1,0:T(8,128)(2,1)} %get-tuple-element.452) | copy-start | bytes 393220 | tf_op jit(solution)/shard_map/while
  83.3 12.0 %copy-start.1 = (f32[1,256]{1,0:T(1,128)S(1)}, f32[1,256]{1,0:T(1,128)}, u32[]{:S(2)}) copy-start(f32[1,256]{1,0:T(1,128)} %get-tuple-element.453) | copy-start | bytes 3076 | tf_op jit(solution)/shard_map/while
  83.4 6.8 %collective-permute-start = (bf16[128,256]{1,0:T(8,128)(2,1)S(1)}, bf16[128,256]{1,0:T(8,128)(2,1)S(1)}, u32[]{:S(2)}, u32[]{:S(2)}) collective-permute-start(bf16[128,256]{1,0:T(8,128)(2,1)S(1)} %get-tuple-element.401), channel_id=1, source_target_pairs={{1,0},{2,1},{3,2},{4,3},{5,4},{6,5},{7,6},{9,8},{10,9},{11,10},{12... | collective-permute-start | bytes 196616 | tf_op jit(solution)/shard_map/while/body/eval_jaxpr/ppermute | solution.py:17
  86.1 7.1 %collective-permute-start.1 = (bf16[128,256]{1,0:T(8,128)(2,1)S(1)}, bf16[128,256]{1,0:T(8,128)(2,1)S(1)}, u32[]{:S(2)}, u32[]{:S(2)}) collective-permute-start(bf16[128,256]{1,0:T(8,128)(2,1)S(1)} %get-tuple-element.402), channel_id=1, source_target_pairs={{0,1},{1,2},{2,3},{3,4},{4,5},{5,6},{6,7},{8,9},{9,10},{10,11},{11... | collective-permute-start | bytes 196616 | tf_op jit(solution)/shard_map/while/body/eval_jaxpr/ppermute | solution.py:14
  96.6 7.0 %collective-permute-start.2 = (bf16[384,256]{1,0:T(8,128)(2,1)S(1)}, bf16[384,256]{1,0:T(8,128)(2,1)S(1)}, u32[]{:S(2)}, u32[]{:S(2)}) collective-permute-start(bf16[384,256]{1,0:T(8,128)(2,1)S(1)} %get-tuple-element.406), channel_id=1, source_target_pairs={{0,8},{8,16},{16,24},{1,9},{9,17},{17,25},{2,10},{10,18},{18,26},{... | collective-permute-start | bytes 589832 | tf_op jit(solution)/shard_map/while/body/eval_jaxpr/ppermute | solution.py:25
  105.3 11.3 %copy-start = (bf16[256,256]{1,0:T(8,128)(2,1)S(1)}, bf16[256,256]{1,0:T(8,128)(2,1)}, u32[]{:S(2)}) copy-start(bf16[256,256]{1,0:T(8,128)(2,1)} %get-tuple-element.452) | copy-start | bytes 393220 | tf_op jit(solution)/shard_map/while
  105.4 6.8 %collective-permute-start = (bf16[128,256]{1,0:T(8,128)(2,1)S(1)}, bf16[128,256]{1,0:T(8,128)(2,1)S(1)}, u32[]{:S(2)}, u32[]{:S(2)}) collective-permute-start(bf16[128,256]{1,0:T(8,128)(2,1)S(1)} %get-tuple-element.401), channel_id=1, source_target_pairs={{1,0},{2,1},{3,2},{4,3},{5,4},{6,5},{7,6},{9,8},{10,9},{11,10},{12... | collective-permute-start | bytes 196616 | tf_op jit(solution)/shard_map/while/body/eval_jaxpr/ppermute | solution.py:17
  107.4 7.1 %collective-permute-start.1 = (bf16[128,256]{1,0:T(8,128)(2,1)S(1)}, bf16[128,256]{1,0:T(8,128)(2,1)S(1)}, u32[]{:S(2)}, u32[]{:S(2)}) collective-permute-start(bf16[128,256]{1,0:T(8,128)(2,1)S(1)} %get-tuple-element.402), channel_id=1, source_target_pairs={{0,1},{1,2},{2,3},{3,4},{4,5},{5,6},{6,7},{8,9},{9,10},{10,11},{11... | collective-permute-start | bytes 196616 | tf_op jit(solution)/shard_map/while/body/eval_jaxpr/ppermute | solution.py:14
  117.8 7.3 %collective-permute-start.2 = (bf16[384,256]{1,0:T(8,128)(2,1)S(1)}, bf16[384,256]{1,0:T(8,128)(2,1)S(1)}, u32[]{:S(2)}, u32[]{:S(2)}) collective-permute-start(bf16[384,256]{1,0:T(8,128)(2,1)S(1)} %get-tuple-element.406), channel_id=1, source_target_pairs={{0,8},{8,16},{16,24},{1,9},{9,17},{17,25},{2,10},{10,18},{18,26},{... | collective-permute-start | bytes 589832 | tf_op jit(solution)/shard_map/while/body/eval_jaxpr/ppermute | solution.py:25
  126.9 6.8 %collective-permute-start = (bf16[128,256]{1,0:T(8,128)(2,1)S(1)}, bf16[128,256]{1,0:T(8,128)(2,1)S(1)}, u32[]{:S(2)}, u32[]{:S(2)}) collective-permute-start(bf16[128,256]{1,0:T(8,128)(2,1)S(1)} %get-tuple-element.401), channel_id=1, source_target_pairs={{1,0},{2,1},{3,2},{4,3},{5,4},{6,5},{7,6},{9,8},{10,9},{11,10},{12... | collective-permute-start | bytes 196616 | tf_op jit(solution)/shard_map/while/body/eval_jaxpr/ppermute | solution.py:17
  129.0 7.1 %collective-permute-start.1 = (bf16[128,256]{1,0:T(8,128)(2,1)S(1)}, bf16[128,256]{1,0:T(8,128)(2,1)S(1)}, u32[]{:S(2)}, u32[]{:S(2)}) collective-permute-start(bf16[128,256]{1,0:T(8,128)(2,1)S(1)} %get-tuple-element.402), channel_id=1, source_target_pairs={{0,1},{1,2},{2,3},{3,4},{4,5},{5,6},{6,7},{8,9},{9,10},{10,11},{11... | collective-permute-start | bytes 196616 | tf_op jit(solution)/shard_map/while/body/eval_jaxpr/ppermute | solution.py:14
  139.4 7.0 %collective-permute-start.2 = (bf16[384,256]{1,0:T(8,128)(2,1)S(1)}, bf16[384,256]{1,0:T(8,128)(2,1)S(1)}, u32[]{:S(2)}, u32[]{:S(2)}) collective-permute-start(bf16[384,256]{1,0:T(8,128)(2,1)S(1)} %get-tuple-element.406), channel_id=1, source_target_pairs={{0,8},{8,16},{16,24},{1,9},{9,17},{17,25},{2,10},{10,18},{18,26},{... | collective-permute-start | bytes 589832 | tf_op jit(solution)/shard_map/while/body/eval_jaxpr/ppermute | solution.py:25
  (3 other events, 34.0 us)
where the time goes:
time: 169 us; the launch traced here: 167 us
  starting transfers between devices  77.8 us (46%)
  waiting for transfers between devices  26.2 us (16%)
  blocking collectives  20.3 us (12%)
  other arithmetic  18.5 us (11%)
  matrix products  18 us (11%)
  local copies, waits for them, and re-layouts  5.61 us (3%)
    ppermute x7, starting transfers between devices, passed_along(): return lax.ppermute(block, axis, route)  36 us
    ppermute x7, starting transfers between devices, extended(): lax.ppermute(lax.slice_in_dim(block, block.shape[dim] - width, None, axis...  24.6 us
    all_to_all x1, blocking collectives, shards(): lax.all_to_all(finished_rows, 'section', split_axis=0, concat_axis=0, til...  20.3 us
    ppermute x7, waiting for transfers between devices, extended(): lax.ppermute(lax.slice_in_dim(block, block.shape[dim] - width, None, axis...  18.9 us
    ppermute x7, starting transfers between devices, extended(): lax.ppermute(lax.slice_in_dim(block, 0, width, axis=dim), axis, backward)  17.2 us
    dot_general x7, matrix products, apply_layer(): jnp.einsum('bkij,bkjf->bif', tile_ones, sources, preferred_element_type=j...  9.84 us
    dot_general x7, matrix products, apply_layer(): jnp.dot(aggregate, layer_weight, preferred_element_type=jnp.float32)  8.2 us
    convert_element_type x7, other arithmetic, apply_layer(): scaled = (current.astype(jnp.float32) * inv_root).astype(jnp.bfloat16)  7.34 us
  transfers between devices with their start and end apart: 21, of which 14 were waited for; matrix products, arithmetic and copies ran while one was open for 3% of the time, Pallas kernels for 0%

commit v1 on v0

v1 whole, which is shorter than its diff:
```python
import functools

import jax
import jax.numpy as jnp
from jax import lax
from jax.experimental import pallas as pl
from jax.experimental.pallas import tpu as pltpu
from jax.sharding import PartitionSpec as P

MESH = pl.DeviceIdType.MESH
REACH = 1
SPAN = 2 * REACH + 1


def kernel(
    sections, slabs, feat, pat, col, deg, w, b, out,
    xcur, pt, amat, own, low, high, wbuf, bbuf,
    load_sem, halo_send, halo_recv, w_send, w_recv, b_send, b_recv, f_send, fb_send,
):
    layers = wbuf.shape[0]
    per_dev, slots, tile = pt.shape[0], pt.shape[1], pt.shape[2]
    sec = lax.axis_index("section")
    slab = lax.axis_index("blk")
    partner = sec + 1 - 2 * (sec % 2)
    pairs = sections // 2
    others = [(sec + 2 * step) % sections for step in range(1, pairs)]

    loads = [
        pltpu.make_async_copy(feat.at[sec], xcur, load_sem.at[0]),
        pltpu.make_async_copy(pat.at[sec], pt, load_sem.at[1]),
        pltpu.make_async_copy(w.at[0], wbuf.at[sec], load_sem.at[2]),
        pltpu.make_async_copy(b, bbuf.at[sec], load_sem.at[3]),
    ]
    for load in loads:
        load.start()

    has_low = slab > 0
    has_high = slab < slabs - 1
    barrier = pltpu.get_barrier_semaphore()
    for peer in [partner] + others:
        pl.semaphore_signal(barrier, inc=1, device_id={"section": peer}, device_id_type=MESH)

    @pl.when(has_low)
    def _():
        pl.semaphore_signal(barrier, inc=1, device_id={"blk": slab - 1}, device_id_type=MESH)

    @pl.when(has_high)
    def _():
        pl.semaphore_signal(barrier, inc=1, device_id={"blk": slab + 1}, device_id_type=MESH)

    row_ids = lax.broadcasted_iota(jnp.int32, (tile, tile), 0)
    col_ids = lax.broadcasted_iota(jnp.int32, (tile, tile), 1)
    eye = jnp.where(row_ids == col_ids, 1.0, 0.0).astype(jnp.float32)

    def rows(i):
        return slice(i * tile, (i + 1) * tile)

    inv_row = lax.rsqrt(deg[pl.ds(sec, 1), :].astype(jnp.float32))
    inv = [jnp.sum(eye * inv_row[:, rows(i)], axis=1, keepdims=True) for i in range(per_dev)]

    loads[0].wait()
    for i in range(per_dev):
        own[0, rows(i), :] = (xcur[rows(i), :].astype(jnp.float32) * inv[i]).astype(jnp.bfloat16)

    @pl.when(jnp.logical_not(has_low))
    def _():
        low[...] = jnp.zeros_like(low)

    @pl.when(jnp.logical_not(has_high))
    def _():
        high[...] = jnp.zeros_like(high)

    pl.semaphore_wait(barrier, pairs + has_low.astype(jnp.int32) + has_high.astype(jnp.int32))

    def to_low(layer):
        return pltpu.make_async_remote_copy(
            src_ref=own.at[layer, rows(0), :], dst_ref=high.at[layer],
            send_sem=halo_send.at[layer, 0], recv_sem=halo_recv.at[layer, 1],
            device_id={"blk": slab - 1}, device_id_type=MESH,
        )

    def to_high(layer):
        return pltpu.make_async_remote_copy(
            src_ref=own.at[layer, rows(per_dev - 1), :], dst_ref=low.at[layer],
            send_sem=halo_send.at[layer, 1], recv_sem=halo_recv.at[layer, 0],
            device_id={"blk": slab + 1}, device_id_type=MESH,
        )

    def send_low(layer):
        @pl.when(has_low)
        def _():
            to_low(layer).start()

    def send_high(layer):
        @pl.when(has_high)
        def _():
            to_high(layer).start()

    def wait_low(layer):
        @pl.when(has_low)
        def _():
            to_high(layer).wait_recv()

    def wait_high(layer):
        @pl.when(has_high)
        def _():
            to_low(layer).wait_recv()

    def weight_copies(src_w, src_b, index, send_w, send_b, peer):
        return [
            pltpu.make_async_remote_copy(
                src_ref=src, dst_ref=buf.at[index], send_sem=ssem, recv_sem=rsem.at[index],
                device_id={"section": peer}, device_id_type=MESH,
            )
            for src, buf, ssem, rsem in (
                (src_w, wbuf, send_w, w_recv), (src_b, bbuf, send_b, b_recv),
            )
        ]

    send_low(0)
    send_high(0)
    own_sends = []
    for n, peer in enumerate(others + [partner]):
        own_sends += weight_copies(w.at[0], b, sec, w_send.at[n], b_send.at[n], peer)
    for copy in own_sends:
        copy.start()

    def forward(layer):
        return weight_copies(
            wbuf.at[layer], bbuf.at[layer], layer, f_send.at[layer], fb_send.at[layer], partner
        )

    passes_on = [
        jnp.logical_and(sec % 2 == layer % 2, sec != layer) for layer in range(layers)
    ]

    def take_weight(layer):
        @pl.when(sec != layer)
        def _():
            for copy in forward(layer):
                copy.wait_recv()

        @pl.when(passes_on[layer])
        def _():
            for copy in forward(layer):
                copy.start()

    loads[1].wait()
    for i in range(per_dev):
        merged = [jnp.zeros((tile, tile), jnp.float32) for _ in range(SPAN)]
        merged[REACH] = eye
        for slot in range(slots):
            ones = pt[i, slot].astype(jnp.float32)
            offset = col[i, sec, slot] - (slab * per_dev + i) + REACH
            for place in range(SPAN):
                merged[place] += ones * jnp.where(offset == place, 1.0, 0.0)
        for place in range(SPAN):
            amat[i, :, rows(place)] = merged[place].astype(jnp.bfloat16)
    loads[2].wait()
    loads[3].wait()

    def dot(x, y):
        return jnp.dot(x, y, preferred_element_type=jnp.float32)

    for layer in range(layers):
        def finish(i, summed):
            aggregate = (summed * inv[i]).astype(jnp.bfloat16)
            hidden = dot(aggregate, wbuf[layer]) + bbuf[layer]
            new = (xcur[rows(i), :].astype(jnp.float32) + jnp.maximum(hidden, 0.0)).astype(jnp.bfloat16)
            if layer == layers - 1:
                out[0, rows(i), :] = new
            else:
                xcur[rows(i), :] = new
                own[layer + 1, rows(i), :] = (new.astype(jnp.float32) * inv[i]).astype(jnp.bfloat16)

        last = per_dev - 1
        first_part = dot(amat[0, :, tile:], own[layer, : 2 * tile, :])
        last_part = dot(amat[last, :, : 2 * tile], own[layer, (last - 1) * tile :, :])
        inner = [dot(amat[i], own[layer, (i - 1) * tile : (i + 2) * tile, :]) for i in range(1, last)]
        take_weight(layer)
        for i in range(1, last):
            finish(i, inner[i - 1])
        wait_low(layer)
        finish(0, first_part + dot(amat[0, :, :tile], low[layer]))
        if layer < layers - 1:
            send_low(layer + 1)
        wait_high(layer)
        finish(last, last_part + dot(amat[last, :, 2 * tile :], high[layer]))
        if layer < layers - 1:
            send_high(layer + 1)

    for copy in own_sends:
        copy.wait_send()
    for layer in range(layers):
        @pl.when(has_low)
        def _():
            to_low(layer).wait_send()

        @pl.when(has_high)
        def _():
            to_high(layer).wait_send()

        @pl.when(passes_on[layer])
        def _():
            for copy in forward(layer):
                copy.wait_send()


def solution(mesh):
    sections, slabs = mesh.shape["section"], mesh.shape["blk"]

    def shards(features, pattern, col_block, degree, weight, bias):
        groups, slab_rows, width = features.shape
        per_dev, slots, tile = pattern.shape[1:4]
        layers = sections * weight.shape[0]
        assert groups == sections and weight.shape[0] == 1 and sections % 2 == 0 and per_dev >= 2
        bf16, f32 = jnp.bfloat16, jnp.float32
        dma = pltpu.SemaphoreType.DMA
        hbm = pl.BlockSpec(memory_space=pl.ANY)
        vmem = pl.BlockSpec(memory_space=pltpu.VMEM)
        peers = sections // 2
        return pl.pallas_call(
            functools.partial(kernel, sections, slabs),
            out_shape=jax.ShapeDtypeStruct((1, slab_rows, width), bf16),
            in_specs=[hbm, hbm, pl.BlockSpec(memory_space=pltpu.SMEM), vmem, hbm, hbm],
            out_specs=vmem,
            scratch_shapes=[
                pltpu.VMEM((slab_rows, width), bf16),
                pltpu.VMEM((per_dev, slots, tile, tile), jnp.int32),
                pltpu.VMEM((per_dev, tile, SPAN * tile), bf16),
                pltpu.VMEM((layers, slab_rows, width), bf16),
                pltpu.VMEM((layers, tile, width), bf16),
                pltpu.VMEM((layers, tile, width), bf16),
                pltpu.VMEM((layers, width, width), bf16),
                pltpu.VMEM((layers, 1, width), f32),
                dma((4,)),
                dma((layers, 2)),
                dma((layers, 2)),
                dma((peers,)),
                dma((layers,)),
                dma((peers,)),
                dma((layers,)),
                dma((layers,)),
                dma((layers,)),
            ],
            compiler_params=pltpu.CompilerParams(collective_id=0, has_side_effects=True),
        )(features, pattern, jnp.transpose(col_block, (1, 0, 2)), degree, weight, bias)

    return jax.shard_map(
        shards,
        mesh=mesh,
        in_specs=(
            P(None, "blk", None),
            P(None, "blk", None, None, None),
            P(None, "blk", None),
            P(None, "blk"),
            P("section", None, None),
            P("section", None),
        ),
        out_specs=P("section", "blk", None),
        check_vma=False,
    )
```

time: 169 us -> 25.7 us (0.15)
  the two profiles are of different devices: /device:TPU:24 before, /device:TPU:18 now
where the time goes in v1:
time: 25.7 us; the launch traced here: 25.5 us
  Pallas kernels  23.9 us (93%)
  local copies, waits for them, and re-layouts  1.62 us (6%)
    pallas_call x1, Pallas kernels, shards(): pl.pallas_call(functools.partial(kernel, sections, slabs), out_shape=jax....  23.9 us
    unnamed x1, local copies, waits for them, and re-layouts  1.62 us

profile of v1, /device:TPU:18, one launch (start us, length us, event | category | flops | bytes accessed | tf_op | source)
XLA Modules:
  0.0 25.5 jit_solution(11272748133922046471)
XLA Ops:
  0.0 23.9 %shard_map.64 = bf16[1,384,256]{2,1,0:T(8,128)(2,1)} custom-call(bf16[4,384,256]{2,1,0:T(8,128)(2,1)} %feat.1, s32[4,3,3,128,128]{4,3,2,1,0:T(8,128)} %pat.1, s32[3,4,3]{2,1,0:T(4,128)} %bitcast.1, s32[4,384]{1,0:T(4,128)} %deg.1, bf16[1,256,256]{2,1,0:T(8,128)(2,1)} %w.1, f32[1,256]{1,0:T(1,128)} %b.1), custom_call_target="tpu_custom_call" | custom-call | tf_op jit(solution)/shard_map/pallas_call | solution.py:222
  23.9 1.6 %copy.8 = bf16[1,384,256]{2,1,0:T(8,128)(2,1)} copy(bf16[1,384,256]{2,1,0:T(8,128)(2,1)} %shard_map.64) | data formatting | bytes 393216

commit v2 on v1

v2 whole, which is shorter than its diff:
```python
import functools

import jax
import jax.numpy as jnp
from jax import lax
from jax.experimental import pallas as pl
from jax.experimental.pallas import tpu as pltpu
from jax.sharding import PartitionSpec as P

MESH = pl.DeviceIdType.MESH
REACH = 1
SPAN = 2 * REACH + 1


def kernel(
    sections, slabs, feat, pat, col, deg, w, b, out,
    xcur, pt, inv, edge_halo, edge_own, inner_adj, own, halo, wbuf, bbuf,
    load_sem, halo_send, halo_recv, w_send, w_recv, b_send, b_recv, f_send, fb_send,
):
    layers = wbuf.shape[0]
    per_dev, slots, tile = pt.shape[0], pt.shape[1], pt.shape[2]
    sec = lax.axis_index("section")
    slab = lax.axis_index("blk")
    partner = sec + 1 - 2 * (sec % 2)
    pairs = sections // 2
    others = [(sec + 2 * step) % sections for step in range(1, pairs)]

    loads = [
        pltpu.make_async_copy(feat.at[sec], xcur, load_sem.at[0]),
        pltpu.make_async_copy(pat.at[sec], pt, load_sem.at[1]),
        pltpu.make_async_copy(w.at[0], wbuf.at[sec], load_sem.at[2]),
        pltpu.make_async_copy(b, bbuf.at[sec], load_sem.at[3]),
    ]
    for load in loads:
        load.start()

    far, near = slab % 2, 1 - slab % 2

    def peer_of(side):
        return slab + 2 * side - 1

    def has(side):
        return jnp.logical_and(peer_of(side) >= 0, peer_of(side) < slabs)

    barrier = pltpu.get_barrier_semaphore()
    for peer in [partner] + others:
        pl.semaphore_signal(barrier, inc=1, device_id={"section": peer}, device_id_type=MESH)

    for side in (far, near):
        @pl.when(has(side))
        def _():
            pl.semaphore_signal(
                barrier, inc=1, device_id={"blk": peer_of(side)}, device_id_type=MESH
            )

    row_ids = lax.broadcasted_iota(jnp.int32, (tile, tile), 0)
    col_ids = lax.broadcasted_iota(jnp.int32, (tile, tile), 1)
    eye = jnp.where(row_ids == col_ids, 1.0, 0.0).astype(jnp.float32)

    def rows(i):
        return slice(i * tile, (i + 1) * tile)

    inv_row = lax.rsqrt(deg[pl.ds(sec, 1), :].astype(jnp.float32))
    for i in range(per_dev):
        column = jnp.sum(eye * inv_row[:, rows(i)], axis=1, keepdims=True)
        inv[rows(i), :] = jnp.broadcast_to(column, (tile, inv.shape[1]))

    loads[0].wait()
    own[0] = (xcur[...].astype(jnp.float32) * inv[...]).astype(jnp.bfloat16)

    for side in (far, near):
        @pl.when(jnp.logical_not(has(side)))
        def _():
            for layer in range(layers):
                halo[layer, side] = jnp.zeros(halo.shape[2:], halo.dtype)

    pl.semaphore_wait(
        barrier, pairs + has(far).astype(jnp.int32) + has(near).astype(jnp.int32)
    )

    last = per_dev - 1

    def edge_rows(side):
        return pl.ds(pl.multiple_of(side * last * tile, tile), tile)

    def edge_pair(side):
        return pl.ds(pl.multiple_of(side * (last - 1) * tile, tile), 2 * tile)

    def halo_copy(layer, side):
        return pltpu.make_async_remote_copy(
            src_ref=own.at[layer, edge_rows(side), :], dst_ref=halo.at[layer, 1 - side],
            send_sem=halo_send.at[layer, side], recv_sem=halo_recv.at[layer, 1 - side],
            device_id={"blk": peer_of(side)}, device_id_type=MESH,
        )

    def arrival(layer, side):
        return pltpu.make_async_remote_copy(
            src_ref=own.at[layer, edge_rows(side), :], dst_ref=halo.at[layer, side],
            send_sem=halo_send.at[layer, side], recv_sem=halo_recv.at[layer, side],
            device_id={"blk": peer_of(side)}, device_id_type=MESH,
        )

    def send(layer, side):
        @pl.when(has(side))
        def _():
            halo_copy(layer, side).start()

    def take(layer, side):
        @pl.when(has(side))
        def _():
            arrival(layer, side).wait_recv()

    def sent(layer, side):
        @pl.when(has(side))
        def _():
            halo_copy(layer, side).wait_send()

    def weight_copies(src_w, src_b, index, send_w, send_b, peer):
        return [
            pltpu.make_async_remote_copy(
                src_ref=src, dst_ref=buf.at[index], send_sem=ssem, recv_sem=rsem.at[index],
                device_id={"section": peer}, device_id_type=MESH,
            )
            for src, buf, ssem, rsem in (
                (src_w, wbuf, send_w, w_recv), (src_b, bbuf, send_b, b_recv),
            )
        ]

    send(0, far)
    send(0, near)
    own_sends = []
    for n, peer in enumerate(others + [partner]):
        own_sends += weight_copies(w.at[0], b, sec, w_send.at[n], b_send.at[n], peer)
    for copy in own_sends:
        copy.start()

    def forward(layer):
        return weight_copies(
            wbuf.at[layer], bbuf.at[layer], layer, f_send.at[layer], fb_send.at[layer], partner
        )

    passes_on = [
        jnp.logical_and(sec % 2 == layer % 2, sec != layer) for layer in range(layers)
    ]

    def take_weight(layer):
        @pl.when(sec != layer)
        def _():
            for copy in forward(layer):
                copy.wait_recv()

        @pl.when(passes_on[layer])
        def _():
            for copy in forward(layer):
                copy.start()

    loads[1].wait()
    for i in range(per_dev):
        merged = [jnp.zeros((tile, tile), jnp.float32) for _ in range(SPAN)]
        merged[REACH] = eye
        for slot in range(slots):
            ones = pt[i, slot].astype(jnp.float32)
            offset = col[i, sec, slot] - (slab * per_dev + i) + REACH
            for place in range(SPAN):
                merged[place] += ones * jnp.where(offset == place, 1.0, 0.0)
        merged = [part.astype(jnp.bfloat16) for part in merged]
        if i == 0:
            edge_halo[0] = merged[0]
            edge_own[0, :, :tile] = merged[1]
            edge_own[0, :, tile:] = merged[2]
        elif i == last:
            edge_own[1, :, :tile] = merged[0]
            edge_own[1, :, tile:] = merged[1]
            edge_halo[1] = merged[2]
        else:
            for place in range(SPAN):
                inner_adj[i - 1, :, rows(place)] = merged[place]
    loads[2].wait()
    loads[3].wait()

    def dot(x, y):
        return jnp.dot(x, y, preferred_element_type=jnp.float32)

    def finish(layer, place, summed):
        scale = inv[place, :]
        aggregate = (summed * scale).astype(jnp.bfloat16)
        hidden = dot(aggregate, wbuf[layer]) + bbuf[layer]
        new = xcur[place, :].astype(jnp.float32) + jnp.maximum(hidden, 0.0)
        new = new.astype(jnp.bfloat16)
        if layer == layers - 1:
            out[0, place, :] = new
        else:
            xcur[place, :] = new
            own[layer + 1, place, :] = (new.astype(jnp.float32) * scale).astype(jnp.bfloat16)

    def edge_part(layer, side):
        return dot(edge_own[side], own[layer, edge_pair(side), :])

    far_part, near_part = edge_part(0, far), edge_part(0, near)
    take_weight(0)
    for layer in range(layers):
        more = layer < layers - 1
        take(layer, far)
        finish(layer, edge_rows(far), far_part + dot(edge_halo[far], halo[layer, far]))
        if more:
            send(layer + 1, far)
        take(layer, near)
        finish(layer, edge_rows(near), near_part + dot(edge_halo[near], halo[layer, near]))
        if more:
            send(layer + 1, near)
        for i in range(1, last):
            inner = dot(inner_adj[i - 1], own[layer, (i - 1) * tile : (i + 2) * tile, :])
            finish(layer, rows(i), inner)
        if more:
            far_part, near_part = edge_part(layer + 1, far), edge_part(layer + 1, near)
            take_weight(layer + 1)

    for copy in own_sends:
        copy.wait_send()
    for layer in range(layers):
        sent(layer, far)
        sent(layer, near)

        @pl.when(passes_on[layer])
        def _():
            for copy in forward(layer):
                copy.wait_send()


def solution(mesh):
    sections, slabs = mesh.shape["section"], mesh.shape["blk"]

    def shards(features, pattern, col_block, degree, weight, bias):
        groups, slab_rows, width = features.shape
        per_dev, slots, tile = pattern.shape[1:4]
        layers = sections * weight.shape[0]
        assert groups == sections and weight.shape[0] == 1 and sections % 2 == 0 and per_dev >= 2
        bf16, f32 = jnp.bfloat16, jnp.float32
        dma = pltpu.SemaphoreType.DMA
        hbm = pl.BlockSpec(memory_space=pl.ANY)
        vmem = pl.BlockSpec(memory_space=pltpu.VMEM)
        peers = sections // 2
        return pl.pallas_call(
            functools.partial(kernel, sections, slabs),
            out_shape=pltpu.VMEM((1, slab_rows, width), bf16),
            in_specs=[hbm, hbm, pl.BlockSpec(memory_space=pltpu.SMEM), vmem, hbm, hbm],
            out_specs=vmem,
            scratch_shapes=[
                pltpu.VMEM((slab_rows, width), bf16),
                pltpu.VMEM((per_dev, slots, tile, tile), jnp.int32),
                pltpu.VMEM((slab_rows, width), f32),
                pltpu.VMEM((2, tile, tile), bf16),
                pltpu.VMEM((2, tile, 2 * tile), bf16),
                pltpu.VMEM((max(per_dev - 2, 1), tile, SPAN * tile), bf16),
                pltpu.VMEM((layers, slab_rows, width), bf16),
                pltpu.VMEM((layers, 2, tile, width), bf16),
                pltpu.VMEM((layers, width, width), bf16),
                pltpu.VMEM((layers, 1, width), f32),
                dma((4,)),
                dma((layers, 2)),
                dma((layers, 2)),
                dma((peers,)),
                dma((layers,)),
                dma((peers,)),
                dma((layers,)),
                dma((layers,)),
                dma((layers,)),
            ],
            compiler_params=pltpu.CompilerParams(collective_id=0, has_side_effects=True),
        )(features, pattern, jnp.transpose(col_block, (1, 0, 2)), degree, weight, bias)

    return jax.shard_map(
        shards,
        mesh=mesh,
        in_specs=(
            P(None, "blk", None),
            P(None, "blk", None, None, None),
            P(None, "blk", None),
            P(None, "blk"),
            P("section", None, None),
            P("section", None),
        ),
        out_specs=P("section", "blk", None),
        check_vma=False,
    )
```

time: 25.7 us -> 22.4 us (0.87)
  Pallas kernels: 23.9 us -> 21.5 us
  local copies, waits for them, and re-layouts: 1.62 us -> 0.68 us
    pallas_call x1, Pallas kernels: 23.9 us -> 21.5 us  [shards(): pl.pallas_call(functools.partial(kernel, sections, slabs), out_shape=pltp...]
    unnamed x1, local copies, waits for them, and re-layouts: 1.62 us -> 0.68 us
where the time goes in v2:
time: 22.4 us; the launch traced here: 22.2 us
  Pallas kernels  21.5 us (96%)
  local copies, waits for them, and re-layouts  0.68 us (3%)
    pallas_call x1, Pallas kernels, shards(): pl.pallas_call(functools.partial(kernel, sections, slabs), out_shape=pltp...  21.5 us
    unnamed x1, local copies, waits for them, and re-layouts  0.68 us

profile of v2, /device:TPU:18, one launch (start us, length us, event | category | flops | bytes accessed | tf_op | source)
XLA Modules:
  0.0 22.2 jit_solution(1273388564417228185)
XLA Ops:
  0.0 21.5 %shard_map.64 = bf16[1,384,256]{2,1,0:T(8,128)(2,1)S(1)} custom-call(bf16[4,384,256]{2,1,0:T(8,128)(2,1)} %feat.1, s32[4,3,3,128,128]{4,3,2,1,0:T(8,128)} %pat.1, s32[3,4,3]{2,1,0:T(4,128)} %bitcast.1, s32[4,384]{1,0:T(4,128)} %deg.1, bf16[1,256,256]{2,1,0:T(8,128)(2,1)} %w.1, f32[1,256]{1,0:T(1,128)} %b.1), custom_call_target="tpu_custom_call" | custom-call | tf_op jit(solution)/shard_map/pallas_call | solution.py:243
  21.5 0.7 %copy.8 = bf16[1,384,256]{2,1,0:T(8,128)(2,1)} copy(bf16[1,384,256]{2,1,0:T(8,128)(2,1)S(1)} %shard_map.64) | data formatting | bytes 393216

commit v3 on v2

--- a/solution.py
+++ b/solution.py
@@ -13,8 +13,8 @@
 
 
 def kernel(
-    sections, slabs, feat, pat, col, deg, w, b, out,
-    xcur, pt, inv, edge_halo, edge_own, inner_adj, own, halo, wbuf, bbuf,
+    sections, slabs, feat, pat, col_hbm, deg_hbm, w, b, out,
+    col, deg, xcur, pt, inv, edge_halo, edge_own, inner_adj, own, halo, wbuf, bbuf,
     load_sem, halo_send, halo_recv, w_send, w_recv, b_send, b_recv, f_send, fb_send,
 ):
     layers = wbuf.shape[0]
@@ -25,6 +25,10 @@
     pairs = sections // 2
     others = [(sec + 2 * step) % sections for step in range(1, pairs)]
 
+    col_load = pltpu.make_async_copy(col_hbm, col, load_sem.at[5])
+    col_load.start()
+    deg_load = pltpu.make_async_copy(deg_hbm, deg, load_sem.at[4])
+    deg_load.start()
     loads = [
         pltpu.make_async_copy(feat.at[sec], xcur, load_sem.at[0]),
         pltpu.make_async_copy(pat.at[sec], pt, load_sem.at[1]),
@@ -60,6 +64,7 @@
     def rows(i):
         return slice(i * tile, (i + 1) * tile)
 
+    deg_load.wait()
     inv_row = lax.rsqrt(deg[pl.ds(sec, 1), :].astype(jnp.float32))
     for i in range(per_dev):
         column = jnp.sum(eye * inv_row[:, rows(i)], axis=1, keepdims=True)
@@ -155,6 +160,7 @@
                 copy.start()
 
     loads[1].wait()
+    col_load.wait()
     for i in range(per_dev):
         merged = [jnp.zeros((tile, tile), jnp.float32) for _ in range(SPAN)]
         merged[REACH] = eye
@@ -243,9 +249,11 @@
         return pl.pallas_call(
             functools.partial(kernel, sections, slabs),
             out_shape=pltpu.VMEM((1, slab_rows, width), bf16),
-            in_specs=[hbm, hbm, pl.BlockSpec(memory_space=pltpu.SMEM), vmem, hbm, hbm],
+            in_specs=[hbm, hbm, hbm, hbm, hbm, hbm],
             out_specs=vmem,
             scratch_shapes=[
+                pltpu.SMEM((per_dev, groups, slots), jnp.int32),
+                pltpu.VMEM(degree.shape, jnp.int32),
                 pltpu.VMEM((slab_rows, width), bf16),
                 pltpu.VMEM((per_dev, slots, tile, tile), jnp.int32),
                 pltpu.VMEM((slab_rows, width), f32),
@@ -256,7 +264,7 @@
                 pltpu.VMEM((layers, 2, tile, width), bf16),
                 pltpu.VMEM((layers, width, width), bf16),
                 pltpu.VMEM((layers, 1, width), f32),
-                dma((4,)),
+                dma((6,)),
                 dma((layers, 2)),
                 dma((layers, 2)),
                 dma((peers,)),

time: 22.4 us -> 21.5 us (0.960)
  Pallas kernels: 21.5 us -> 20.7 us
    pallas_call x1, Pallas kernels: 21.5 us -> 20.7 us  [shards(): pl.pallas_call(functools.partial(kernel, sections, slabs), out_shape=pltp...]
where the time goes in v3:
time: 21.5 us; the launch traced here: 21.4 us
  Pallas kernels  20.7 us (96%)
  local copies, waits for them, and re-layouts  0.68 us (3%)
    pallas_call x1, Pallas kernels, shards(): pl.pallas_call(functools.partial(kernel, sections, slabs), out_shape=pltp...  20.7 us
    unnamed x1, local copies, waits for them, and re-layouts  0.68 us

profile of v3, /device:TPU:18, one launch (start us, length us, event | category | flops | bytes accessed | tf_op | source)
XLA Modules:
  0.0 21.4 jit_solution(2926191994927779312)
XLA Ops:
  0.0 20.7 %shard_map.64 = bf16[1,384,256]{2,1,0:T(8,128)(2,1)S(1)} custom-call(bf16[4,384,256]{2,1,0:T(8,128)(2,1)} %feat.1, s32[4,3,3,128,128]{4,3,2,1,0:T(8,128)} %pat.1, s32[3,4,3]{2,1,0:T(4,128)} %bitcast.1, s32[4,384]{1,0:T(4,128)} %deg_hbm.1, bf16[1,256,256]{2,1,0:T(8,128)(2,1)} %w.1, f32[1,256]{1,0:T(1,128)} %b.1), custom_call_target="tpu_custom_call" | custom-call | tf_op jit(solution)/shard_map/pallas_call | solution.py:249
  20.7 0.7 %copy.8 = bf16[1,384,256]{2,1,0:T(8,128)(2,1)} copy(bf16[1,384,256]{2,1,0:T(8,128)(2,1)S(1)} %shard_map.64) | data formatting | bytes 393216

commit v4 on v3

--- a/solution.py
+++ b/solution.py
@@ -25,6 +25,25 @@
     pairs = sections // 2
     others = [(sec + 2 * step) % sections for step in range(1, pairs)]
 
+    far, near = slab % 2, 1 - slab % 2
+
+    def peer_of(side):
+        return slab + 2 * side - 1
+
+    def has(side):
+        return jnp.logical_and(peer_of(side) >= 0, peer_of(side) < slabs)
+
+    barrier = pltpu.get_barrier_semaphore()
+    for peer in [partner] + others:
+        pl.semaphore_signal(barrier, inc=1, device_id={"section": peer}, device_id_type=MESH)
+
+    for side in (far, near):
+        @pl.when(has(side))
+        def _():
+            pl.semaphore_signal(
+                barrier, inc=1, device_id={"blk": peer_of(side)}, device_id_type=MESH
+            )
+
     col_load = pltpu.make_async_copy(col_hbm, col, load_sem.at[5])
     col_load.start()
     deg_load = pltpu.make_async_copy(deg_hbm, deg, load_sem.at[4])
@@ -38,25 +57,6 @@
     for load in loads:
         load.start()
 
-    far, near = slab % 2, 1 - slab % 2
-
-    def peer_of(side):
-        return slab + 2 * side - 1
-
-    def has(side):
-        return jnp.logical_and(peer_of(side) >= 0, peer_of(side) < slabs)
-
-    barrier = pltpu.get_barrier_semaphore()
-    for peer in [partner] + others:
-        pl.semaphore_signal(barrier, inc=1, device_id={"section": peer}, device_id_type=MESH)
-
-    for side in (far, near):
-        @pl.when(has(side))
-        def _():
-            pl.semaphore_signal(
-                barrier, inc=1, device_id={"blk": peer_of(side)}, device_id_type=MESH
-            )
-
     row_ids = lax.broadcasted_iota(jnp.int32, (tile, tile), 0)
     col_ids = lax.broadcasted_iota(jnp.int32, (tile, tile), 1)
     eye = jnp.where(row_ids == col_ids, 1.0, 0.0).astype(jnp.float32)
@@ -71,7 +71,8 @@
         inv[rows(i), :] = jnp.broadcast_to(column, (tile, inv.shape[1]))
 
     loads[0].wait()
-    own[0] = (xcur[...].astype(jnp.float32) * inv[...]).astype(jnp.bfloat16)
+    for i in (0, per_dev - 1):
+        own[0, rows(i), :] = (xcur[rows(i), :].astype(jnp.float32) * inv[rows(i), :]).astype(jnp.bfloat16)
 
     for side in (far, near):
         @pl.when(jnp.logical_not(has(side)))
@@ -133,6 +134,8 @@
 
     send(0, far)
     send(0, near)
+    for i in range(1, last):
+        own[0, rows(i), :] = (xcur[rows(i), :].astype(jnp.float32) * inv[rows(i), :]).astype(jnp.bfloat16)
     own_sends = []
     for n, peer in enumerate(others + [partner]):
         own_sends += weight_copies(w.at[0], b, sec, w_send.at[n], b_send.at[n], peer)
@@ -199,6 +202,11 @@
             xcur[place, :] = new
             own[layer + 1, place, :] = (new.astype(jnp.float32) * scale).astype(jnp.bfloat16)
 
+    def inner_rows(layer):
+        for i in range(1, last):
+            inner = dot(inner_adj[i - 1], own[layer, (i - 1) * tile : (i + 2) * tile, :])
+            finish(layer, rows(i), inner)
+
     def edge_part(layer, side):
         return dot(edge_own[side], own[layer, edge_pair(side), :])
 
@@ -206,6 +214,8 @@
     take_weight(0)
     for layer in range(layers):
         more = layer < layers - 1
+        if not more:
+            inner_rows(layer)
         take(layer, far)
         finish(layer, edge_rows(far), far_part + dot(edge_halo[far], halo[layer, far]))
         if more:
@@ -214,9 +224,8 @@
         finish(layer, edge_rows(near), near_part + dot(edge_halo[near], halo[layer, near]))
         if more:
             send(layer + 1, near)
-        for i in range(1, last):
-            inner = dot(inner_adj[i - 1], own[layer, (i - 1) * tile : (i + 2) * tile, :])
-            finish(layer, rows(i), inner)
+        if more:
+            inner_rows(layer)
         if more:
             far_part, near_part = edge_part(layer + 1, far), edge_part(layer + 1, near)
             take_weight(layer + 1)

time: 21.5 us -> 21.4 us (level)
  no operation moved by 1% of the time
where the time goes in v4:
time: 21.4 us; the launch traced here: 21.2 us
  Pallas kernels  20.5 us (96%)
  local copies, waits for them, and re-layouts  0.68 us (3%)
    pallas_call x1, Pallas kernels, shards(): pl.pallas_call(functools.partial(kernel, sections, slabs), out_shape=pltp...  20.5 us
    unnamed x1, local copies, waits for them, and re-layouts  0.68 us

profile of v4, /device:TPU:18, one launch (start us, length us, event | category | flops | bytes accessed | tf_op | source)
XLA Modules:
  0.0 21.2 jit_solution(11191873297035018390)
XLA Ops:
  0.0 20.5 %shard_map.64 = bf16[1,384,256]{2,1,0:T(8,128)(2,1)S(1)} custom-call(bf16[4,384,256]{2,1,0:T(8,128)(2,1)} %feat.1, s32[4,3,3,128,128]{4,3,2,1,0:T(8,128)} %pat.1, s32[3,4,3]{2,1,0:T(4,128)} %bitcast.1, s32[4,384]{1,0:T(4,128)} %deg_hbm.1, bf16[1,256,256]{2,1,0:T(8,128)(2,1)} %w.1, f32[1,256]{1,0:T(1,128)} %b.1), custom_call_target="tpu_custom_call" | custom-call | tf_op jit(solution)/shard_map/pallas_call | solution.py:258
  20.5 0.7 %copy.8 = bf16[1,384,256]{2,1,0:T(8,128)(2,1)} copy(bf16[1,384,256]{2,1,0:T(8,128)(2,1)S(1)} %shard_map.64) | data formatting | bytes 393216
